TPU v7x, 32 devices: a whole 2x2x4 slice. The times are simulated.
32 devices in a mesh: dp: 32 (over z, y, x, core).
Axes of the slice: x: 2, y: 2, z: 4, core: 2. Of those that a mesh axis runs over, the one named last changes fastest.
Arguments:
- grads: bfloat16 [64, 1024, 1024], P('dp'), may hold values from -6 to 6
- memory: bfloat16 [64, 1024, 1024], P('dp'), may hold values from -6 to 6
- block_ids: int32 [16], replicated, may hold values from 0 to 63, as said below
- layer_ids: int32 [16], replicated, may hold values from 0 to 1, as said below
- master: float32 [128, 16384], P(None, 'dp'), may hold values from -8 to 8
- first_moment: float32 [128, 16384], P(None, 'dp'), may hold values from -8 to 8
- second_moment: float32 [128, 16384], P(None, 'dp'), may hold values from 0.25 to 4
Outputs:
- new_memory: bfloat16 [64, 1024, 1024], P('dp')
- master_new: float32 [128, 16384], P(None, 'dp')
- first_new: float32 [128, 16384], P(None, 'dp')
- second_new: float32 [128, 16384], P(None, 'dp')
- step_blocks: bfloat16 [16, 16384], replicated
Inputs may be any that keep to these rules, and one draw needn't show every extreme that they name: Block ids number the 64 tiles of a layer, and the pairs (layer_ids[k], block_ids[k]) are distinct. `layer_ids`: every layer is named by at least a quarter of the 16 entries, rounded down.
All inputs are finite; a program needn't handle non-finite values.
Results may differ from a plain program's by a relative error of at most 0.0004.
Values may be sent and summed in bfloat16 or wider, within the bound.
A program may use at most 64 MiB of HBM per device.

v0:
```python
import jax
import jax.numpy as jnp
from jax import lax
from jax.sharding import PartitionSpec as P

TILE = 128
filter_rate = 0.3
beta_one = 0.9
beta_two = 0.999
adam_eps = 1e-06
weight_decay = 0.01
learn_rate = 0.01
norm_eps = 1e-06


def take_tiles(source, layer_ids, tile_row, tile_col):

    def single(layer_id, row_tile, col_tile):
        return lax.dynamic_slice(
            source, (layer_id, row_tile * TILE, col_tile * TILE), (1, TILE, TILE)
        )[0]

    return jax.vmap(single)(layer_ids, tile_row, tile_col)


def pack_blocks(grads_dev, memory_dev, layer_ids, tile_row, tile_col):
    grad_tiles = take_tiles(grads_dev, layer_ids, tile_row, tile_col).astype(jnp.float32)
    memory_tiles = take_tiles(memory_dev, layer_ids, tile_row, tile_col).astype(jnp.float32)
    combined = grad_tiles + memory_tiles
    return combined.reshape(combined.shape[0], TILE * TILE)


def selected_mask(layer_ids, block_ids, layers, tile_count):
    columns = layer_ids * (tile_count * tile_count) + block_ids
    all_columns = jnp.arange(layers * tile_count * tile_count, dtype=jnp.int32)
    chosen = jnp.any(columns[:, None] == all_columns[None, :], axis=0)
    return chosen.reshape(layers, tile_count, 1, tile_count, 1)


def filter_memory(grads_dev, memory_dev, chosen):
    layers, model_width, _ = grads_dev.shape
    tile_count = model_width // TILE
    accumulated = grads_dev.astype(jnp.float32) + memory_dev.astype(jnp.float32)
    shaped = accumulated.reshape(layers, tile_count, TILE, tile_count, TILE)
    filtered = jnp.where(chosen, jnp.float32(0.0), shaped).reshape(layers, model_width, model_width)
    mixed = (1.0 - filter_rate) * memory_dev.astype(jnp.float32) + filter_rate * filtered
    return mixed.astype(jnp.bfloat16)


def adam_rows(summed, weights_sel, first_old, second_old):
    first_sel = beta_one * first_old + (1.0 - beta_one) * summed
    second_sel = beta_two * second_old + (1.0 - beta_two) * summed * summed
    update = first_sel / (jnp.sqrt(second_sel) + adam_eps) + weight_decay * weights_sel
    return (first_sel, second_sel, update)


def layer_squares(member, values):
    return jnp.sum(member * jnp.sum(values * values, axis=1)[:, None], axis=0)


def trust_rows(member, weight_total, update_total):
    trust_ratio = jnp.sqrt(weight_total / (update_total + norm_eps))
    return jnp.sum(member * trust_ratio[None, :], axis=1)


def on_device(grads, memory, block_ids, layer_ids, master, first_moment, second_moment):
    layers, model_width, _ = grads.shape
    tile_count = model_width // TILE
    tile_row = block_ids // tile_count
    tile_col = block_ids % tile_count
    columns = layer_ids * (tile_count * tile_count) + block_ids
    member = (layer_ids[:, None] == jnp.arange(layers, dtype=jnp.int32)[None, :]).astype(
        jnp.float32
    )
    weights_sel = jnp.take(master, columns, axis=0)
    first_old = jnp.take(first_moment, columns, axis=0)
    second_old = jnp.take(second_moment, columns, axis=0)
    packed = pack_blocks(grads, memory, layer_ids, tile_row, tile_col)
    summed = lax.psum_scatter(packed, "dp", scatter_dimension=1, tiled=True)
    first_sel, second_sel, update = adam_rows(summed, weights_sel, first_old, second_old)
    weight_total, update_total = lax.psum(
        (layer_squares(member, weights_sel), layer_squares(member, update)), "dp"
    )
    scaled = trust_rows(member, weight_total, update_total)[:, None] * update
    step_blocks = lax.all_gather(scaled.astype(jnp.bfloat16), "dp", axis=1, tiled=True)
    new_memory = filter_memory(
        grads, memory, selected_mask(layer_ids, block_ids, layers, tile_count)
    )
    master_new = master.at[columns].set(weights_sel - learn_rate * scaled)
    first_new = first_moment.at[columns].set(first_sel)
    second_new = second_moment.at[columns].set(second_sel)
    return (new_memory, master_new, first_new, second_new, step_blocks)


def solution(mesh):
    in_specs = (
        P("dp", None, None),
        P("dp", None, None),
        P(),
        P(),
        P(None, "dp"),
        P(None, "dp"),
        P(None, "dp"),
    )
    out_specs = (P("dp", None, None), P(None, "dp"), P(None, "dp"), P(None, "dp"), P())
    return jax.shard_map(
        on_device, mesh=mesh, in_specs=in_specs, out_specs=out_specs, check_vma=False
    )
```

profile of v0, /device:TPU:0, one launch (start us, length us, event | category | flops | bytes accessed | tf_op | source)
XLA Modules:
  0.0 355.8 jit_solution(294397355076881631)
XLA Ops:
  7.2 1.0 copy.36
  8.2 1.0 copy.38
  9.1 0.9 copy.37
  10.1 0.7 fusion.20
  10.9 56.7 %while.3 = (s32[]{:T(128)}, bf16[2,1024,1024]{2,1,0:T(8,128)(2,1)}, s32[16,3]{0,1:T(4,128)S(1)}, bf16[16,1,128,128]{3,2,1,0:T(8,128)(2,1)S(1)}, s32[]{:T(128)}) while((s32[]{:T(128)}, bf16[2,1024,1024]{2,1,0:T(8,128)(2,1)}, s32[16,3]{0,1:T(4,128)S(1)}, bf16[16,1,128,128]{3,2,1,0:T(8,128)(2,1)S(1)}, s32[]{:T(128)}) %tuple.46), condition=%wide.while_cond.1, body=%wide.while_body.1.sunk | while | flops 2 | bytes 65673 | solution.py:19
  11.5 2.9 bitcast_dynamic-update-slice_fusion.5
  15.1 2.9 bitcast_dynamic-update-slice_fusion.5
  18.6 2.9 bitcast_dynamic-update-slice_fusion.5
  22.2 2.9 bitcast_dynamic-update-slice_fusion.5
  25.2 0.5 fusion.30
  25.7 2.9 bitcast_dynamic-update-slice_fusion.5
  28.7 0.5 fusion.30
  29.2 2.9 bitcast_dynamic-update-slice_fusion.5
  32.3 0.5 fusion.30
  32.8 2.9 bitcast_dynamic-update-slice_fusion.5
  35.8 0.5 fusion.30
  36.3 2.9 bitcast_dynamic-update-slice_fusion.5
  39.4 0.5 fusion.30
  39.9 2.9 bitcast_dynamic-update-slice_fusion.5
  43.4 2.9 bitcast_dynamic-update-slice_fusion.5
  47.0 2.9 bitcast_dynamic-update-slice_fusion.5
  50.5 2.9 bitcast_dynamic-update-slice_fusion.5
  54.1 2.9 bitcast_dynamic-update-slice_fusion.5
  57.1 0.5 fusion.30
  57.6 2.9 bitcast_dynamic-update-slice_fusion.5
  60.6 0.5 fusion.30
  61.1 2.9 bitcast_dynamic-update-slice_fusion.5
  64.1 0.5 fusion.30
  64.7 2.9 bitcast_dynamic-update-slice_fusion.5
  67.7 56.7 %while.2 = (s32[]{:T(128)}, bf16[2,1024,1024]{2,1,0:T(8,128)(2,1)}, s32[16,3]{0,1:T(4,128)S(1)}, bf16[16,1,128,128]{3,2,1,0:T(8,128)(2,1)S(1)}, s32[]{:T(128)}) while((s32[]{:T(128)}, bf16[2,1024,1024]{2,1,0:T(8,128)(2,1)}, s32[16,3]{0,1:T(4,128)S(1)}, bf16[16,1,128,128]{3,2,1,0:T(8,128)(2,1)S(1)}, s32[]{:T(128)}) %tuple.56), condition=%wide.while_cond, body=%wide.while_body.sunk | while | flops 2 | bytes 65673 | solution.py:19
  67.8 0.5 fusion.29
  68.3 2.9 bitcast_dynamic-update-slice_fusion.4
  71.9 2.9 bitcast_dynamic-update-slice_fusion.4
  75.4 2.9 bitcast_dynamic-update-slice_fusion.4
  79.0 2.9 bitcast_dynamic-update-slice_fusion.4
  82.5 2.9 bitcast_dynamic-update-slice_fusion.4
  86.1 2.9 bitcast_dynamic-update-slice_fusion.4
  89.1 0.5 fusion.29
  89.6 2.9 bitcast_dynamic-update-slice_fusion.4
  92.6 0.5 fusion.29
  93.2 2.9 bitcast_dynamic-update-slice_fusion.4
  96.7 2.9 bitcast_dynamic-update-slice_fusion.4
  100.2 2.9 bitcast_dynamic-update-slice_fusion.4
  103.8 2.9 bitcast_dynamic-update-slice_fusion.4
  107.3 2.9 bitcast_dynamic-update-slice_fusion.4
  110.9 2.9 bitcast_dynamic-update-slice_fusion.4
  114.4 2.9 bitcast_dynamic-update-slice_fusion.4
  117.9 2.9 bitcast_dynamic-update-slice_fusion.4
  121.5 2.9 bitcast_dynamic-update-slice_fusion.4
  124.6 1.6 copy.14
  126.4 1.9 broadcast_in_dim.51
  128.4 5.3 %broadcast_in_dim.52 = pred[2,1024,1024]{2,1,0:T(8,128)(4,1)S(1)} reshape(pred[2,8,128,8,128]{4,3,2,1,0:T(8,128)(4,1)} %broadcast_in_dim.51) | data formatting | bytes 4194304 | tf_op jit(solution)/shard_map/jit(_where)/broadcast_in_dim | solution.py:45
  133.6 0.6 gather_fusion
  134.2 0.6 gather_fusion.2
  134.8 0.6 gather_fusion.1
  135.4 6.2 %fusion.1 = bf16[2,1024,1024]{2,1,0:T(8,128)(2,1)} fusion(bf16[2,1024,1024]{2,1,0:T(8,128)(2,1)} %get-tuple-element.159, pred[2,1024,1024]{2,1,0:T(8,128)(4,1)S(1)} %broadcast_in_dim.52, bf16[2,1024,1024]{2,1,0:T(8,128)(2,1)} %get-tuple-element.160), kind=kLoop, calls=%fused_computation.13 | loop fusion | flops 16777216 | bytes 14680064 | tf_op jit(solution)/shard_map/convert_element_type | solution.py:47
  141.6 124.0 %reduce-scatter.2.cloned.1.call-done = f32[16,512]{1,0:T(8,128)} async-done(((f32[16,16384]{1,0:T(8,128)}), f32[16,512]{1,0:T(8,128)}) %reduce-scatter.2.cloned.1.call-update) | async-done | bytes 32784 | tf_op jit(solution)/shard_map/reduce_scatter | solution.py:79
  265.6 1.0 multiply_reduce_fusion
  266.7 36.9 %all-reduce = (f32[2]{0:T(128)S(1)}, f32[2]{0:T(128)S(1)}) all-reduce(f32[2]{0:T(128)S(1)} %get-tuple-element.23, f32[2]{0:T(128)S(1)} %get-tuple-element.22), channel_id=1, replica_groups=mesh['dp'=32] {'dp'}, use_global_device_ids=true, to_apply=%region_3.5 | all-reduce | flops 4 | bytes 32 | tf_op jit(solution)/shard_map/psum | solution.py:81
  303.7 41.3 %all_gather.3 = bf16[16,16384]{1,0:T(8,128)(2,1)S(1)} all-gather(bf16[16,512]{1,0:T(8,128)(2,1)S(1)} %multiply_convert_fusion), channel_id=1, replica_groups=mesh['dp'=32] {'dp'}, dimensions={1}, use_global_device_ids=true | all-gather | bytes 540672 | tf_op jit(solution)/shard_map/all_gather | solution.py:85
  345.0 0.8 scatter_custom_fusion
  345.9 1.1 scatter_custom_fusion.1
  347.0 1.1 scatter_custom_fusion.2
  348.1 0.8 copy.40
  (78 shorter events, 14.3 us)
Async XLA Ops:
  7.2 258.4 %reduce-scatter.2.cloned.1.call-start = ((), (), s32[]{:S(2)}) async-start(), calls=%async_computation.1 | async-start | bytes 1081344 | tf_op jit(solution)/shard_map/reduce_scatter | solution.py:79
  8.2 118.0 %copy-start.3 = (s32[16]{0:T(128)S(1)}, s32[16]{0:T(128)}, u32[]{:S(2)}) copy-start(s32[16]{0:T(128)} %param.12) | copy-start | bytes 196
  8.2 118.0 %copy-start.4 = (s32[16]{0:T(128)S(1)}, s32[16]{0:T(128)}, u32[]{:S(2)}) copy-start(s32[16]{0:T(128)} %param.11) | copy-start | bytes 196
  345.8 3.1 copy-start.2
  347.0 2.0 copy-start.1
  348.1 0.9 copy-start
Sparse Core Ops, SparseCore 0:
  126.3 139.2 reduce-scatter.1
where the time goes:
time: 359 us; the launch traced here: 356 us
  local copies, waits for them, and re-layouts  127 us (35%)
  waiting for transfers between devices  124 us (35%)
  blocking collectives  78.1 us (22%)
  between operations  14.2 us (4%)
  other arithmetic  11.5 us (3%)
    reduce_scatter x1, waiting for transfers between devices, on_device(): summed = lax.psum_scatter(packed, 'dp', scatter_dimension=1, tiled=True)  124 us
    gather x96, local copies, waits for them, and re-layouts  113 us
    all_gather x1, blocking collectives, on_device(): lax.all_gather(scaled.astype(jnp.bfloat16), 'dp', axis=1, tiled=True)  41.3 us
    psum x1, blocking collectives, on_device(): lax.psum((layer_squares(member, weights_sel), layer_squares(member, updat...  36.9 us
    broadcast_in_dim x3, local copies, waits for them, and re-layouts, filter_memory(): jnp.where(chosen, jnp.float32(0.0), shaped)  7.3 us
  transfers between devices with their start and end apart: 1, of which 1 were waited for; matrix products, arithmetic and copies ran while one was open for 4% of the time, Pallas kernels for 0%

commit v1 on v0

--- a/solution.py
+++ b/solution.py
@@ -82,7 +82,12 @@
         (layer_squares(member, weights_sel), layer_squares(member, update)), "dp"
     )
     scaled = trust_rows(member, weight_total, update_total)[:, None] * update
-    step_blocks = lax.all_gather(scaled.astype(jnp.bfloat16), "dp", axis=1, tiled=True)
+    shard = scaled.astype(jnp.bfloat16)
+    size = lax.axis_size("dp")
+    repeats = [size if d == 1 else 1 for d in range(shard.ndim)]
+    step_blocks = lax.all_to_all(
+        jnp.tile(shard, repeats), "dp", split_axis=1, concat_axis=1, tiled=True
+    )
     new_memory = filter_memory(
         grads, memory, selected_mask(layer_ids, block_ids, layers, tile_count)
     )

time: 359 us -> 337 us (0.939)
  blocking collectives: 78.1 us -> 36.9 us
  waiting for transfers between devices: 124 us -> 138 us
  starting transfers between devices: 0.04 us -> 5.06 us
    all_gather x1 -> x0, blocking collectives: 41.3 us -> none  [on_device(): lax.all_gather(scaled.astype(jnp.bfloat16), 'dp', axis=1, tiled=True)]
    reduce_scatter x1, waiting for transfers between devices: 124 us -> 138 us  [on_device(): summed = lax.psum_scatter(packed, 'dp', scatter_dimension=1, tiled=True)]
    all_to_all x0 -> x1, starting transfers between devices: none -> 5.02 us  [on_device(): lax.all_to_all(jnp.tile(shard, repeats), 'dp', split_axis=1, concat_axis=...]
  transfers between devices with their start and end apart: 1 -> 2, of which waited for: 1 -> 1; matrix products, arithmetic and copies ran while one was open for 4% -> 5% of each run, Pallas kernels for 0% -> 0%
where the time goes in v1:
time: 337 us; the launch traced here: 334 us
  waiting for transfers between devices  138 us (41%)
  local copies, waits for them, and re-layouts  128 us (38%)
  blocking collectives  36.9 us (11%)
  between operations  14.2 us (4%)
  other arithmetic  11.2 us (3%)
  starting transfers between devices  5.06 us (2%)
    reduce_scatter x1, waiting for transfers between devices, on_device(): summed = lax.psum_scatter(packed, 'dp', scatter_dimension=1, tiled=True)  138 us
    gather x96, local copies, waits for them, and re-layouts  113 us
    psum x1, blocking collectives, on_device(): lax.psum((layer_squares(member, weights_sel), layer_squares(member, updat...  36.9 us
    broadcast_in_dim x3, local copies, waits for them, and re-layouts, filter_memory(): jnp.where(chosen, jnp.float32(0.0), shaped)  7.3 us
  transfers between devices with their start and end apart: 2, of which 1 were waited for; matrix products, arithmetic and copies ran while one was open for 5% of the time, Pallas kernels for 0%

profile of v1, /device:TPU:0, one launch (start us, length us, event | category | flops | bytes accessed | tf_op | source)
XLA Modules:
  0.0 333.8 jit_solution(5854893425249265329)
XLA Ops:
  7.2 1.0 copy.38
  8.2 1.0 copy.40
  9.1 0.9 copy.39
  10.1 0.7 fusion.20
  10.9 56.7 %while.3 = (s32[]{:T(128)}, bf16[2,1024,1024]{2,1,0:T(8,128)(2,1)}, s32[16,3]{0,1:T(4,128)S(1)}, bf16[16,1,128,128]{3,2,1,0:T(8,128)(2,1)S(1)}, s32[]{:T(128)}) while((s32[]{:T(128)}, bf16[2,1024,1024]{2,1,0:T(8,128)(2,1)}, s32[16,3]{0,1:T(4,128)S(1)}, bf16[16,1,128,128]{3,2,1,0:T(8,128)(2,1)S(1)}, s32[]{:T(128)}) %tuple.46), condition=%wide.while_cond.1, body=%wide.while_body.1.sunk | while | flops 2 | bytes 65673 | solution.py:19
  11.5 2.9 bitcast_dynamic-update-slice_fusion.5
  15.1 2.9 bitcast_dynamic-update-slice_fusion.5
  18.6 2.9 bitcast_dynamic-update-slice_fusion.5
  22.2 2.9 bitcast_dynamic-update-slice_fusion.5
  25.2 0.5 fusion.30
  25.7 2.9 bitcast_dynamic-update-slice_fusion.5
  28.7 0.5 fusion.30
  29.2 2.9 bitcast_dynamic-update-slice_fusion.5
  32.3 0.5 fusion.30
  32.8 2.9 bitcast_dynamic-update-slice_fusion.5
  35.8 0.5 fusion.30
  36.3 2.9 bitcast_dynamic-update-slice_fusion.5
  39.4 0.5 fusion.30
  39.9 2.9 bitcast_dynamic-update-slice_fusion.5
  43.4 2.9 bitcast_dynamic-update-slice_fusion.5
  47.0 2.9 bitcast_dynamic-update-slice_fusion.5
  50.5 2.9 bitcast_dynamic-update-slice_fusion.5
  54.1 2.9 bitcast_dynamic-update-slice_fusion.5
  57.1 0.5 fusion.30
  57.6 2.9 bitcast_dynamic-update-slice_fusion.5
  60.6 0.5 fusion.30
  61.1 2.9 bitcast_dynamic-update-slice_fusion.5
  64.1 0.5 fusion.30
  64.7 2.9 bitcast_dynamic-update-slice_fusion.5
  67.7 56.7 %while.2 = (s32[]{:T(128)}, bf16[2,1024,1024]{2,1,0:T(8,128)(2,1)}, s32[16,3]{0,1:T(4,128)S(1)}, bf16[16,1,128,128]{3,2,1,0:T(8,128)(2,1)S(1)}, s32[]{:T(128)}) while((s32[]{:T(128)}, bf16[2,1024,1024]{2,1,0:T(8,128)(2,1)}, s32[16,3]{0,1:T(4,128)S(1)}, bf16[16,1,128,128]{3,2,1,0:T(8,128)(2,1)S(1)}, s32[]{:T(128)}) %tuple.54), condition=%wide.while_cond, body=%wide.while_body.sunk | while | flops 2 | bytes 65673 | solution.py:19
  67.8 0.5 fusion.29
  68.3 2.9 bitcast_dynamic-update-slice_fusion.4
  71.9 2.9 bitcast_dynamic-update-slice_fusion.4
  75.4 2.9 bitcast_dynamic-update-slice_fusion.4
  79.0 2.9 bitcast_dynamic-update-slice_fusion.4
  82.5 2.9 bitcast_dynamic-update-slice_fusion.4
  86.1 2.9 bitcast_dynamic-update-slice_fusion.4
  89.1 0.5 fusion.29
  89.6 2.9 bitcast_dynamic-update-slice_fusion.4
  93.2 2.9 bitcast_dynamic-update-slice_fusion.4
  96.7 2.9 bitcast_dynamic-update-slice_fusion.4
  100.2 2.9 bitcast_dynamic-update-slice_fusion.4
  103.8 2.9 bitcast_dynamic-update-slice_fusion.4
  107.3 2.9 bitcast_dynamic-update-slice_fusion.4
  110.9 2.9 bitcast_dynamic-update-slice_fusion.4
  114.4 2.9 bitcast_dynamic-update-slice_fusion.4
  117.9 2.9 bitcast_dynamic-update-slice_fusion.4
  121.5 2.9 bitcast_dynamic-update-slice_fusion.4
  124.6 1.6 copy.17
  126.2 0.6 gather_fusion
  126.8 0.6 gather_fusion.2
  127.4 0.6 gather_fusion.1
  128.0 137.6 %reduce-scatter.2.cloned.1.call-done = f32[16,512]{1,0:T(8,128)} async-done(((f32[16,16384]{1,0:T(8,128)}), f32[16,512]{1,0:T(8,128)}) %reduce-scatter.2.cloned.1.call-update) | async-done | bytes 32784 | tf_op jit(solution)/shard_map/reduce_scatter | solution.py:79
  265.6 1.0 multiply_reduce_fusion
  266.7 36.9 %all-reduce = (f32[2]{0:T(128)S(1)}, f32[2]{0:T(128)S(1)}) all-reduce(f32[2]{0:T(128)S(1)} %get-tuple-element.23, f32[2]{0:T(128)S(1)} %get-tuple-element.22), channel_id=1, replica_groups=mesh['dp'=32] {'dp'}, use_global_device_ids=true, to_apply=%region_3.5 | all-reduce | flops 4 | bytes 32 | tf_op jit(solution)/shard_map/psum | solution.py:81
  303.7 0.9 tile.2
  304.6 5.0 %all-to-all-start = ((bf16[16,32,512]{2,0,1:T(8,128)(2,1)}), bf16[16,32,512]{2,0,1:T(8,128)(2,1)S(1)}, u32[]{:S(2)}, u32[]{:S(2)}) async-start(bf16[16,32,512]{2,0,1:T(8,128)(2,1)} %tile.2), calls=%async_computation.1 | async-start | bytes 1048576 | tf_op jit(solution)/shard_map/all_to_all | solution.py:88
  309.8 1.9 broadcast_in_dim.51
  311.7 5.3 %broadcast_in_dim.52 = pred[2,1024,1024]{2,1,0:T(8,128)(4,1)S(1)} reshape(pred[2,8,128,8,128]{4,3,2,1,0:T(8,128)(4,1)} %broadcast_in_dim.51) | data formatting | bytes 4194304 | tf_op jit(solution)/shard_map/jit(_where)/broadcast_in_dim | solution.py:45
  317.0 6.2 %fusion.1 = bf16[2,1024,1024]{2,1,0:T(8,128)(2,1)} fusion(bf16[2,1024,1024]{2,1,0:T(8,128)(2,1)} %get-tuple-element.149, pred[2,1024,1024]{2,1,0:T(8,128)(4,1)S(1)} %broadcast_in_dim.52, bf16[2,1024,1024]{2,1,0:T(8,128)(2,1)} %get-tuple-element.150), kind=kLoop, calls=%fused_computation.13 | loop fusion | flops 16777216 | bytes 14680064 | tf_op jit(solution)/shard_map/convert_element_type | solution.py:47
  323.2 1.1 scatter_custom_fusion
  324.3 0.9 scatter_custom_fusion.1
  325.2 0.9 scatter_custom_fusion.2
  326.1 0.9 copy.14
  (84 shorter events, 14.8 us)
Async XLA Ops:
  7.2 258.4 %reduce-scatter.2.cloned.1.call-start = ((), (), s32[]{:S(2)}) async-start(), calls=%async_computation.2 | async-start | bytes 1081344 | tf_op jit(solution)/shard_map/reduce_scatter | solution.py:79
  8.2 118.0 %copy-start.5 = (s32[16]{0:T(128)S(1)}, s32[16]{0:T(128)}, u32[]{:S(2)}) copy-start(s32[16]{0:T(128)} %param.12) | copy-start | bytes 196
  8.2 118.0 %copy-start.6 = (s32[16]{0:T(128)S(1)}, s32[16]{0:T(128)}, u32[]{:S(2)}) copy-start(s32[16]{0:T(128)} %param.11) | copy-start | bytes 196
  266.5 45.2 %copy-start.4 = (f32[16,512]{1,0:T(8,128)}, f32[16,512]{1,0:T(8,128)S(1)}, u32[]{:S(2)}) copy-start(f32[16,512]{1,0:T(8,128)S(1)} %get-tuple-element.43) | copy-start | bytes 98308
  304.6 21.5 %all-to-all-start = ((bf16[16,32,512]{2,0,1:T(8,128)(2,1)}), bf16[16,32,512]{2,0,1:T(8,128)(2,1)S(1)}, u32[]{:S(2)}, u32[]{:S(2)}) async-start(bf16[16,32,512]{2,0,1:T(8,128)(2,1)} %tile.2), calls=%async_computation.1 | async-start | bytes 1048576 | tf_op jit(solution)/shard_map/all_to_all | solution.py:88
  317.0 7.3 %copy-start.3 = (f32[16,512]{1,0:T(8,128)S(1)}, f32[16,512]{1,0:T(8,128)}, u32[]{:S(2)}) copy-start(f32[16,512]{1,0:T(8,128)} %reduce-scatter.2.cloned.1.call-done) | copy-start | bytes 98308
  324.3 2.6 copy-start.2
  325.2 1.8 copy-start.1
  326.1 0.9 copy-start
Sparse Core Ops, SparseCore 0:
  126.3 139.2 reduce-scatter.1
